TPU v7x, 32 devices: a whole 2x2x4 slice. The times are simulated.
32 devices in a mesh: grp: 2 (over x), seq: 8 (over z, y), col: 2 (over core).
Axes of the slice: x: 2, y: 2, z: 4, core: 2. Of those that a mesh axis runs over, the one named last changes fastest.
Arguments:
- signal: bfloat16 [8192, 1408], P(('grp', 'seq'), 'col'), parts along dimension 0, may hold values from -6 to 6
- conv_weight: bfloat16 [5, 1408, 1408], P(None, None, 'col'), may hold values from -0.15625 to 0.15625
- conv_gain: float32 [1408], replicated, may hold values from 0.1 to 1.9
- embed_weight: bfloat16 [1408, 1536], P('col', 'seq'), may hold values from -0.15625 to 0.15625
- attn_gain: float32 [1536], replicated, may hold values from 0.1 to 1.9
- query_weight: bfloat16 [1536, 1024], P('seq'), may hold values from -4 to 4
- keyvalue_weight: bfloat16 [1536, 320], P('seq'), may hold values from -4 to 4
- output_weight: bfloat16 [1536, 1536], P(None, 'seq'), may hold values from -0.15625 to 0.15625
- rowcol_weight: bfloat16 [1536, 256], replicated, may hold values from -0.15625 to 0.15625
- pair_weight: bfloat16 [128, 128], replicated, may hold values from -0.5 to 0.5
Outputs:
- tokens: bfloat16 [2048, 1536], P(('grp', 'seq', 'col')), parts along dimension 0
- pair_out: bfloat16 [128, 64, 128], P(('grp', 'seq'), 'col'), parts along dimension 0
There are 2 independent parts, one for each index of `grp`. A program takes and returns all parts, laid end to end along the dimension named above; an argument that names none is the same for every part. Nothing has to cross between parts.
All inputs are finite; a program needn't handle non-finite values.
Results may differ from a plain program's by a relative error of at most 0.015.
Values may be sent and summed in bfloat16 or wider, within the bound.
A program may use at most 128 MiB of HBM per device.

v0:
```python
import jax
import jax.numpy as jnp
from jax import lax
from jax.sharding import PartitionSpec as P

DK = 128
DV = 192
POOL = 4
PAIR_POOL = 16


def with_halo(array, sides, width):
    for axis, dim in sides:
        size, length = (lax.axis_size(axis), array.shape[dim])
        up = [(i, (i + 1) % size) for i in range(size - 1)]
        down = [(j, i) for i, j in up]
        last = lax.slice_in_dim(array, length - width, length, axis=dim)
        first = lax.slice_in_dim(array, 0, width, axis=dim)
        before = lax.ppermute(last, axis, up)
        after = lax.ppermute(first, axis, down)
        array = jnp.concatenate([before, array, after], axis=dim)
    return array


def rms_scale(values, gain_vector):
    return (
        values * lax.rsqrt(jnp.mean(values * values, axis=-1, keepdims=True) + 1e-06) * gain_vector
    )


def attention_parts(queries, head_count):
    query_rows = queries.reshape(queries.shape[0] * head_count, DK)

    def absorb(running, pieces, first_row):
        running_max, running_sum, accumulated = running
        key_piece, value_piece = pieces
        scores = lax.dot_general(
            query_rows, key_piece, (((1,), (1,)), ((), ())), preferred_element_type=jnp.float32
        )
        newest_max = jnp.maximum(running_max, jnp.max(scores, axis=1))
        weights = jnp.exp(scores - newest_max[:, None])
        running_sum = jnp.sum(weights, axis=1)
        accumulated = jnp.dot(
            weights.astype(jnp.bfloat16), value_piece, preferred_element_type=jnp.float32
        )
        return (newest_max, running_sum, accumulated)

    row_count = query_rows.shape[0]
    initial = (
        jnp.full((row_count,), -1e30, jnp.float32),
        jnp.zeros((row_count,), jnp.float32),
        jnp.zeros((row_count, DV), jnp.float32),
    )
    return (absorb, initial)


def finish_attention(result, token_count):
    running_max, running_sum, accumulated = result
    return (accumulated / running_sum[:, None]).astype(jnp.bfloat16).reshape(token_count, -1)


def on_device(
    signal,
    conv_weight,
    conv_gain,
    embed_weight,
    attn_gain,
    query_weight,
    keyvalue_weight,
    output_weight,
    rowcol_weight,
    pair_weight,
):
    positions = signal.shape[0]
    tap_count = conv_weight.shape[0]
    halo_width = tap_count // 2
    padded = with_halo(signal, (("seq", 0),), halo_width)
    widened = lax.all_gather(padded, "col", axis=1, tiled=True)
    activated = jax.nn.gelu(
        rms_scale(widened.astype(jnp.float32), conv_gain), approximate=True
    ).astype(jnp.bfloat16)
    summed = signal.astype(jnp.float32)
    for tap_index in range(tap_count):
        summed = summed + jnp.dot(
            activated[tap_index : tap_index + positions],
            conv_weight[tap_index],
            preferred_element_type=jnp.float32,
        )
    pooled = jnp.mean(summed.reshape(positions // POOL, POOL, -1), axis=1).astype(jnp.bfloat16)
    embed_full = lax.all_gather(embed_weight, "seq", axis=1, tiled=True)
    col_count = lax.axis_size("col")
    embedded = lax.psum_scatter(
        jnp.dot(pooled, embed_full, preferred_element_type=jnp.float32).astype(jnp.bfloat16),
        "col",
        scatter_dimension=0,
        tiled=True,
    )
    normed = rms_scale(embedded.astype(jnp.float32), attn_gain).astype(jnp.bfloat16)
    head_count = query_weight.shape[1] // DK
    scaling = DK ** (-0.5)
    col_index = lax.axis_index("col")
    local_heads = head_count // col_count
    group_tokens = lax.all_gather(normed, "col", axis=0, tiled=True)
    group_count = group_tokens.shape[0]
    query_half = lax.dynamic_slice_in_dim(
        query_weight, col_index * local_heads * DK, local_heads * DK, 1
    )
    query_sum = jnp.dot(
        group_tokens,
        lax.all_gather(query_half, "seq", axis=0, tiled=True),
        preferred_element_type=jnp.float32,
    )
    keyvalue_sum = jnp.dot(
        group_tokens,
        lax.all_gather(keyvalue_weight, "seq", axis=0, tiled=True),
        preferred_element_type=jnp.float32,
    )
    queries = (query_sum * scaling).astype(jnp.bfloat16)
    keyvalue = keyvalue_sum.astype(jnp.bfloat16)
    absorb, initial = attention_parts(queries, local_heads)
    result = absorb(
        initial,
        (
            lax.all_gather(keyvalue[:, :DK], "seq", axis=0, tiled=True),
            lax.all_gather(keyvalue[:, DK:], "seq", axis=0, tiled=True),
        ),
        jnp.int32(0),
    )
    attended = finish_attention(result, group_count)
    output_half = lax.dynamic_slice_in_dim(
        output_weight, col_index * local_heads * DV, local_heads * DV, 0
    )
    partial_out = jnp.dot(
        attended,
        lax.all_gather(output_half, "seq", axis=1, tiled=True),
        preferred_element_type=jnp.float32,
    )
    attention_out = lax.psum_scatter(
        partial_out.astype(jnp.bfloat16), "col", scatter_dimension=0, tiled=True
    ).astype(jnp.float32)
    tokens = (embedded.astype(jnp.float32) + attention_out).astype(jnp.bfloat16)
    pair_pool = jnp.mean(
        tokens.astype(jnp.float32).reshape(-1, PAIR_POOL, tokens.shape[1]), axis=1
    ).astype(jnp.bfloat16)
    projected = jnp.dot(pair_pool, rowcol_weight, preferred_element_type=jnp.float32).astype(
        jnp.bfloat16
    )
    features = pair_weight.shape[0]
    row_block = lax.all_gather(projected, "col", axis=0, tiled=True)
    column_all = lax.all_gather(row_block[:, features:], "seq", axis=0, tiled=True)
    row_part = row_block[:, :features]
    column_span = column_all.shape[0] // col_count
    column_part = lax.dynamic_slice_in_dim(
        column_all, lax.axis_index("col") * column_span, column_span, 0
    )
    hidden = jax.nn.gelu(
        row_part.astype(jnp.float32)[:, None, :] + column_part.astype(jnp.float32)[None, :, :],
        approximate=True,
    ).astype(jnp.bfloat16)
    pair_out = jnp.dot(
        hidden.reshape(-1, features), pair_weight, preferred_element_type=jnp.float32
    ).astype(jnp.bfloat16)
    return (tokens, pair_out.reshape(row_part.shape[0], column_span, features))


def solution(mesh):
    placed = (
        P(("grp", "seq"), "col"),
        P(None, None, "col"),
        P(),
        P("col", "seq"),
        P(),
        P("seq", None),
        P("seq", None),
        P(None, "seq"),
        P(),
        P(),
    )
    return jax.shard_map(
        on_device,
        mesh=mesh,
        in_specs=placed,
        out_specs=(P(("grp", "seq", "col"), None), P(("grp", "seq"), "col", None)),
        check_vma=False,
    )
```

profile of v0, /device:TPU:0, one launch (start us, length us, event | category | flops | bytes accessed | tf_op | source)
XLA Modules:
  0.0 256.0 jit_solution(12248278608278916954)
XLA Ops:
  7.2 1.4 copy.19
  8.7 4.9 %collective-permute-start = (bf16[2,704]{1,0:T(2,128)(2,1)S(1)}, bf16[2,704]{1,0:T(2,128)(2,1)S(1)}, u32[]{:S(2)}, u32[]{:S(2)}) collective-permute-start(bf16[2,704]{1,0:T(2,128)(2,1)S(1)} %get-tuple-element.4), channel_id=1, source_target_pairs={{0,2},{2,4},{4,6},{6,8},{8,10},{10,12},{12,14},{1,3},{3,5},{5,7},{... | collective-permute-start | bytes 8456 | tf_op jit(solution)/shard_map/ppermute | solution.py:19
  13.6 1.3 collective-permute-start.1
  14.9 4.2 %collective-permute-done.1 = bf16[2,704]{1,0:T(2,128)(2,1)S(1)} collective-permute-done((bf16[2,704]{1,0:T(2,128)(2,1)S(1)}, bf16[2,704]{1,0:T(2,128)(2,1)S(1)}, u32[]{:S(2)}, u32[]{:S(2)}) %collective-permute-start.1) | collective-permute-done | bytes 2848 | tf_op jit(solution)/shard_map/ppermute | solution.py:20
  19.1 1.1 maximum_bitcast_fusion
  20.3 0.7 all-gather.7.cloned.1.call-update
  21.0 10.3 %all-gather.13.cloned.1.call-done = bf16[2,704,516]{1,2,0:T(8,128)(2,1)} async-done(((bf16[1,704,516]{1,2,0:T(8,128)(2,1)}), bf16[2,704,516]{1,2,0:T(8,128)(2,1)}) %all-gather.13.cloned.1.call-update) | async-done | bytes 1453072 | tf_op jit(solution)/shard_map/all_gather | solution.py:78
  31.4 4.3 %copy.22 = f32[2,704,516]{1,0,2:T(2,128)} copy(bf16[2,704,516]{1,2,0:T(8,128)(2,1)} %all-gather.13.cloned.1.call-done) | data formatting | bytes 4359168 | tf_op jit(solution)/shard_map/convert_element_type | solution.py:80
  35.6 5.3 %reshape.62 = f32[1408,516]{0,1:T(8,128)} reshape(f32[2,704,516]{1,0,2:T(2,128)} %copy.22) | data formatting | bytes 5812224 | tf_op jit(solution)/shard_map/convert_element_type | solution.py:80
  41.0 2.4 multiply_reduce_fusion
  43.4 0.5 copy-done.1
  43.9 1.2 fusion.7
  45.1 3.0 %fusion.16 = f32[512,704]{0,1:T(8,128)S(1)} fusion(bf16[5,1408,704]{1,2,0:T(8,128)(2,1)} %param.11, bf16[516,1408]{1,0:T(8,128)(2,1)S(1)} %fusion.7), kind=kOutput, calls=%fused_computation.21 | convolution fusion | flops 1015021568 | bytes 4866048 | tf_op jit(solution)/shard_map/dot_general | solution.py:84
  48.1 1.4 copy-done.4
  49.6 1.3 fusion.12
  50.9 1.3 fusion.10
  52.2 1.3 fusion.8
  53.6 1.5 add_add_fusion
  55.1 1.6 copy.23
  56.7 1.8 reshape.50
  58.5 0.9 reduce_sum.46
  59.5 27.1 %all-gather.7.cloned.1.call-done = bf16[704,1536]{0,1:T(8,128)(2,1)} async-done(((bf16[704,192]{0,1:T(8,128)(2,1)}), bf16[704,1536]{0,1:T(8,128)(2,1)}) %all-gather.7.cloned.1.call-update) | async-done | bytes 2162704 | tf_op jit(solution)/shard_map/all_gather | solution.py:90
  86.6 3.3 %convolution_convert_fusion.1 = bf16[128,1536]{1,0:T(8,128)(2,1)} fusion(bf16[704,1536]{0,1:T(8,128)(2,1)} %all-gather.7.cloned.1.call-done, f32[128,704]{1,0:T(8,128)S(1)} %reduce_sum.46), kind=kOutput, calls=%fused_computation.11 | convolution fusion | flops 277200896 | bytes 2916352 | tf_op jit(solution)/shard_map/dot_general | solution.py:93
  90.0 0.7 constant_dynamic-slice_fusion.1
  90.7 0.8 constant_dynamic-slice_fusion
  91.6 34.7 %all_gather.34 = bf16[1536,320]{1,0:T(8,128)(2,1)S(1)} all-gather(bf16[192,320]{1,0:T(8,128)(2,1)S(1)} %copy-done.6), channel_id=1, replica_groups=mesh['grp'=2,'seq'=8,'col'=2] {'seq'}, dimensions={0}, use_global_device_ids=true | all-gather | bytes 1105920 | tf_op jit(solution)/shard_map/all_gather | solution.py:115
  126.3 1.1 fusion.39
  127.3 1.0 fusion.41
  128.4 2.3 all_gather.32
  130.7 0.5 convolution_convert_fusion.2
  131.2 17.2 %all-gather.9.cloned.1.call-done = bf16[1536,512]{1,0:T(8,128)(2,1)} async-done(((bf16[192,512]{1,0:T(8,128)(2,1)}), bf16[1536,512]{1,0:T(8,128)(2,1)}) %all-gather.9.cloned.1.call-update) | async-done | bytes 1572880 | tf_op jit(solution)/shard_map/all_gather | solution.py:110
  148.5 1.8 fusion.35
  150.3 0.1 reshape.51
  150.4 27.6 %all_gather.35 = bf16[1024,128]{0,1:T(8,128)(2,1)S(1)} all-gather(bf16[128,128]{0,1:T(8,128)(2,1)S(1)} %slice.71), channel_id=1, replica_groups=mesh['grp'=2,'seq'=8,'col'=2] {'seq'}, dimensions={0}, use_global_device_ids=true | all-gather | bytes 294912 | tf_op jit(solution)/shard_map/all_gather | solution.py:124
  177.9 29.5 %all_gather.36 = bf16[1024,192]{0,1:T(8,128)(2,1)S(1)} all-gather(bf16[128,192]{0,1:T(8,128)(2,1)S(1)} %slice.72), channel_id=1, replica_groups=mesh['grp'=2,'seq'=8,'col'=2] {'seq'}, dimensions={0}, use_global_device_ids=true | all-gather | bytes 442368 | tf_op jit(solution)/shard_map/all_gather | solution.py:125
  207.5 0.5 fusion.57
  208.0 0.5 fusion.23
  208.5 0.6 fusion.34
  209.1 0.1 copy.24
  209.2 0.3 reshape.52
  209.6 3.3 %convolution_convert_fusion = bf16[128,1536]{1,0:T(8,128)(2,1)} fusion(bf16[128,768]{1,0:T(8,128)(2,1)S(1)} %reshape.52, bf16[768,1536]{0,1:T(8,128)(2,1)} %all-gather.11.cloned.1.call-done), kind=kOutput, calls=%fused_computation.10 | convolution fusion | flops 302186496 | bytes 2949120 | tf_op jit(solution)/shard_map/dot_general | solution.py:133
  212.9 5.2 %reduce-scatter.5.cloned.1.call-done = bf16[64,1536]{1,0:T(8,128)(2,1)} async-done(((bf16[128,1536]{1,0:T(8,128)(2,1)}), bf16[64,1536]{1,0:T(8,128)(2,1)}) %reduce-scatter.5.cloned.1.call-update) | async-done | bytes 196624 | tf_op jit(solution)/shard_map/reduce_scatter | solution.py:138
  218.1 1.7 convert_reduce_fusion
  219.8 0.2 fusion.36
  220.0 1.8 all-gather.1
  221.9 26.4 %all_gather.39 = bf16[64,128]{1,0:T(8,128)(2,1)S(1)} all-gather(bf16[8,128]{1,0:T(8,128)(2,1)S(1)} %get-tuple-element.7), channel_id=1, replica_groups=mesh['grp'=2,'seq'=8,'col'=2] {'seq'}, dimensions={0}, use_global_device_ids=true | all-gather | bytes 18432 | tf_op jit(solution)/shard_map/all_gather | solution.py:150
  248.3 0.1 fusion.51
  248.4 0.8 convolution_convert_fusion.3
  (44 shorter events, 0.5 us)
Async XLA Ops:
  7.2 212.6 %copy-start = (bf16[1536,256]{1,0:T(8,128)(2,1)S(1)}, bf16[1536,256]{1,0:T(8,128)(2,1)}, u32[]{:S(2)}) copy-start(bf16[1536,256]{1,0:T(8,128)(2,1)} %param.18) | copy-start | bytes 2359300
  7.2 24.2 %all-gather.13.cloned.1.call-start = ((), (), s32[]{:S(2)}) async-start(), calls=%async_computation.7 | async-start | bytes 2396160 | tf_op jit(solution)/shard_map/all_gather | solution.py:78
  8.7 6.2 %collective-permute-start = (bf16[2,704]{1,0:T(2,128)(2,1)S(1)}, bf16[2,704]{1,0:T(2,128)(2,1)S(1)}, u32[]{:S(2)}, u32[]{:S(2)}) collective-permute-start(bf16[2,704]{1,0:T(2,128)(2,1)S(1)} %get-tuple-element.4), channel_id=1, source_target_pairs={{0,2},{2,4},{4,6},{6,8},{8,10},{10,12},{12,14},{1,3},{3,5},{5,7},{... | collective-permute-start | bytes 8456 | tf_op jit(solution)/shard_map/ppermute | solution.py:19
  13.6 5.5 %collective-permute-start.1 = (bf16[2,704]{1,0:T(2,128)(2,1)S(1)}, bf16[2,704]{1,0:T(2,128)(2,1)S(1)}, u32[]{:S(2)}, u32[]{:S(2)}) collective-permute-start(bf16[2,704]{1,0:T(2,128)(2,1)S(1)} %get-tuple-element.5), channel_id=1, source_target_pairs={{2,0},{4,2},{6,4},{8,6},{10,8},{12,10},{14,12},{3,1},{5,3},{7,5},{... | collective-permute-start | bytes 8456 | tf_op jit(solution)/shard_map/ppermute | solution.py:20
  20.2 66.3 %all-gather.7.cloned.1.call-start = ((), (), s32[]{:S(2)}) async-start(), calls=%async_computation.2 | async-start | bytes 2654208 | tf_op jit(solution)/shard_map/all_gather | solution.py:90
  21.0 105.3 %reduce-scatter.3.cloned.1.call-start = ((), (), s32[]{:S(2)}) async-start(), calls=%async_computation.3 | async-start | bytes 589824 | tf_op jit(solution)/shard_map/reduce_scatter | solution.py:92
  41.0 2.9 %copy-start.1 = (f32[1408,516]{0,1:T(8,128)S(1)}, f32[1408,516]{0,1:T(8,128)}, u32[]{:S(2)}) copy-start(f32[1408,516]{0,1:T(8,128)} %reshape.62) | copy-start | bytes 8718340
  41.0 2.9 %copy-start.9 = (f32[1408]{0:T(1024)S(1)}, f32[1408]{0:T(1024)}, u32[]{:S(2)}) copy-start(f32[1408]{0:T(1024)} %param.12) | copy-start | bytes 16900
  45.1 4.4 %copy-start.4 = (bf16[5,1408,704]{1,2,0:T(8,128)(2,1)S(1)}, bf16[5,1408,704]{1,2,0:T(8,128)(2,1)}, u32[]{:S(2)}) copy-start(bf16[5,1408,704]{1,2,0:T(8,128)(2,1)} %param.11) | copy-start | bytes 29736964
  52.2 1.4 copy-start.2
  59.4 30.5 %copy-start.7 = (bf16[192,1024]{1,0:T(8,128)(2,1)S(1)}, bf16[192,1024]{1,0:T(8,128)(2,1)}, u32[]{:S(2)}) copy-start(bf16[192,1024]{1,0:T(8,128)(2,1)} %param.15) | copy-start | bytes 1179652
  59.4 31.3 %copy-start.5 = (bf16[1536,192]{0,1:T(8,128)(2,1)S(1)}, bf16[1536,192]{0,1:T(8,128)(2,1)}, u32[]{:S(2)}) copy-start(bf16[1536,192]{0,1:T(8,128)(2,1)} %param.17) | copy-start | bytes 1769476
  59.4 32.1 %copy-start.6 = (bf16[192,320]{1,0:T(8,128)(2,1)S(1)}, bf16[192,320]{1,0:T(8,128)(2,1)}, u32[]{:S(2)}) copy-start(bf16[192,320]{1,0:T(8,128)(2,1)} %param.16) | copy-start | bytes 368644
  89.9 37.5 %copy-start.10 = (f32[1536]{0:T(1024)S(1)}, f32[1536]{0:T(1024)}, u32[]{:S(2)}) copy-start(f32[1536]{0:T(1024)} %param.14) | copy-start | bytes 18436
  89.9 58.6 %all-gather.9.cloned.1.call-start = ((), (), s32[]{:S(2)}) async-start(), calls=%async_computation.4 | async-start | bytes 1769472 | tf_op jit(solution)/shard_map/all_gather | solution.py:110
  90.7 118.9 %all-gather.11.cloned.1.call-start = ((), (), s32[]{:S(2)}) async-start(), calls=%async_computation.5 | async-start | bytes 2654208 | tf_op jit(solution)/shard_map/all_gather | solution.py:135
  91.5 126.6 %reduce-scatter.5.cloned.1.call-start = ((), (), s32[]{:S(2)}) async-start(), calls=%async_computation.6 | async-start | bytes 589824 | tf_op jit(solution)/shard_map/reduce_scatter | solution.py:138
  209.2 8.9 %copy-start.3 = (bf16[64,1536]{1,0:T(8,128)(2,1)S(1)}, bf16[64,1536]{1,0:T(8,128)(2,1)}, u32[]{:S(2)}) copy-start(bf16[64,1536]{1,0:T(8,128)(2,1)} %reduce-scatter.3.cloned.1.call-done) | copy-start | bytes 589828
  209.5 38.8 %copy-start.8 = (bf16[128,128]{1,0:T(8,128)(2,1)S(1)}, bf16[128,128]{1,0:T(8,128)(2,1)}, u32[]{:S(2)}) copy-start(bf16[128,128]{1,0:T(8,128)(2,1)} %param.19) | copy-start | bytes 98308
Sparse Core Ops, SparseCore 0:
  20.3 10.9 all-gather.12
  33.5 52.9 all-gather.6
  90.0 6.3 reduce-scatter.2
  99.0 49.4 all-gather.8
  150.5 55.1 all-gather.10
  213.0 5.0 reduce-scatter.4
where the time goes:
time: 257 us; the launch traced here: 256 us
  blocking collectives  122 us (47%)
  waiting for transfers between devices  64.9 us (25%)
  matrix products  19.5 us (8%)
  local copies, waits for them, and re-layouts  18.4 us (7%)
  between operations  14.4 us (6%)
  other arithmetic  10.1 us (4%)
  starting transfers between devices  6.43 us (3%)
    all_gather x1, blocking collectives, on_device(): lax.all_gather(keyvalue_weight, 'seq', axis=0, tiled=True)  34.7 us
    all_gather x1, blocking collectives, on_device(): lax.all_gather(keyvalue[:, DK:], 'seq', axis=0, tiled=True)  29.5 us
    all_gather x1, blocking collectives, on_device(): lax.all_gather(keyvalue[:, :DK], 'seq', axis=0, tiled=True)  27.6 us
    all_gather x1, waiting for transfers between devices, on_device(): embed_full = lax.all_gather(embed_weight, 'seq', axis=1, tiled=True)  27.1 us
    all_gather x1, blocking collectives, on_device(): lax.all_gather(row_block[:, features:], 'seq', axis=0, tiled=True)  26.4 us
    all_gather x1, waiting for transfers between devices, on_device(): lax.all_gather(query_half, 'seq', axis=0, tiled=True)  17.2 us
    all_gather x1, waiting for transfers between devices, on_device(): widened = lax.all_gather(padded, 'col', axis=1, tiled=True)  10.3 us
    convert_element_type x2, local copies, waits for them, and re-layouts, on_device(): widened.astype(jnp.float32)  9.6 us
  transfers between devices with their start and end apart: 8, of which 5 were waited for; matrix products, arithmetic and copies ran while one was open for 13% of the time, Pallas kernels for 0%

commit v1 on v0

--- a/solution.py
+++ b/solution.py
@@ -107,7 +107,9 @@
     )
     query_sum = jnp.dot(
         group_tokens,
-        lax.all_gather(query_half, "seq", axis=0, tiled=True),
+        jnp.concatenate(
+            lax.all_to_all(jnp.stack([query_half] * lax.axis_size("seq")), "seq", 0, 0), axis=0
+        ),
         preferred_element_type=jnp.float32,
     )
     keyvalue_sum = jnp.dot(

time: 257 us -> 278 us (1.082)
  blocking collectives: 122 us -> 158 us
  waiting for transfers between devices: 64.9 us -> 47.7 us
  starting transfers between devices: 6.43 us -> 10.1 us
    all_gather x1, blocking collectives: 34.7 us -> 73.4 us  [on_device(): lax.all_gather(keyvalue_weight, 'seq', axis=0, tiled=True)]
    all_gather x1 -> x0, waiting for transfers between devices: 17.2 us -> none  [on_device(): lax.all_gather(query_half, 'seq', axis=0, tiled=True)]
    all_to_all x0 -> x1, starting transfers between devices: none -> 3.71 us  [on_device(): lax.all_to_all(jnp.stack([query_half] * lax.axis_size('seq')), 'seq', 0, 0)]
  transfers between devices with their start and end apart: 8 -> 8, of which waited for: 5 -> 4; matrix products, arithmetic and copies ran while one was open for 13% -> 12% of each run, Pallas kernels for 0% -> 0%
where the time goes in v1:
time: 278 us
  blocking collectives  158 us (57%)
  waiting for transfers between devices  47.7 us (17%)
  local copies, waits for them, and re-layouts  19.2 us (7%)
  matrix products  19.1 us (7%)
  between operations  14.1 us (5%)
  starting transfers between devices  10.1 us (4%)
  other arithmetic  10.1 us (4%)
    all_gather x1, blocking collectives, on_device(): lax.all_gather(keyvalue_weight, 'seq', axis=0, tiled=True)  73.4 us
    all_gather x1, blocking collectives, on_device(): lax.all_gather(keyvalue[:, DK:], 'seq', axis=0, tiled=True)  27.3 us
    all_gather x1, waiting for transfers between devices, on_device(): embed_full = lax.all_gather(embed_weight, 'seq', axis=1, tiled=True)  27.2 us
    all_gather x1, blocking collectives, on_device(): lax.all_gather(keyvalue[:, :DK], 'seq', axis=0, tiled=True)  26.4 us
    all_gather x1, blocking collectives, on_device(): lax.all_gather(row_block[:, features:], 'seq', axis=0, tiled=True)  26.4 us
    all_gather x1, waiting for transfers between devices, on_device(): widened = lax.all_gather(padded, 'col', axis=1, tiled=True)  10.3 us
    convert_element_type x2, local copies, waits for them, and re-layouts, on_device(): widened.astype(jnp.float32)  9.6 us
    dot_general x5, matrix products, on_device(): jnp.dot(activated[tap_index:tap_index + positions], conv_weight[tap_index...  8.47 us
  transfers between devices with their start and end apart: 8, of which 4 were waited for; matrix products, arithmetic and copies ran while one was open for 12% of the time, Pallas kernels for 0%

profile of v1, /device:TPU:0, one launch (start us, length us, event | category | flops | bytes accessed | tf_op | source)
XLA Modules:
  0.0 277.9 jit_solution(1666252651280441231)
XLA Ops:
  7.2 1.4 copy.19
  8.7 4.9 %collective-permute-start = (bf16[2,704]{1,0:T(2,128)(2,1)S(1)}, bf16[2,704]{1,0:T(2,128)(2,1)S(1)}, u32[]{:S(2)}, u32[]{:S(2)}) collective-permute-start(bf16[2,704]{1,0:T(2,128)(2,1)S(1)} %get-tuple-element.4), channel_id=1, source_target_pairs={{0,2},{2,4},{4,6},{6,8},{8,10},{10,12},{12,14},{1,3},{3,5},{5,7},{... | collective-permute-start | bytes 8456 | tf_op jit(solution)/shard_map/ppermute | solution.py:19
  13.6 1.3 collective-permute-start.1
  14.9 4.2 %collective-permute-done.1 = bf16[2,704]{1,0:T(2,128)(2,1)S(1)} collective-permute-done((bf16[2,704]{1,0:T(2,128)(2,1)S(1)}, bf16[2,704]{1,0:T(2,128)(2,1)S(1)}, u32[]{:S(2)}, u32[]{:S(2)}) %collective-permute-start.1) | collective-permute-done | bytes 2848 | tf_op jit(solution)/shard_map/ppermute | solution.py:20
  19.1 1.1 maximum_bitcast_fusion
  20.3 0.7 all-gather.6.cloned.1.call-update
  21.0 10.3 %all-gather.10.cloned.1.call-done = bf16[2,704,516]{1,2,0:T(8,128)(2,1)} async-done(((bf16[1,704,516]{1,2,0:T(8,128)(2,1)}), bf16[2,704,516]{1,2,0:T(8,128)(2,1)}) %all-gather.10.cloned.1.call-update) | async-done | bytes 1453072 | tf_op jit(solution)/shard_map/all_gather | solution.py:78
  31.4 4.3 %copy.22 = f32[2,704,516]{1,0,2:T(2,128)} copy(bf16[2,704,516]{1,2,0:T(8,128)(2,1)} %all-gather.10.cloned.1.call-done) | data formatting | bytes 4359168 | tf_op jit(solution)/shard_map/convert_element_type | solution.py:80
  35.6 5.3 %reshape.68 = f32[1408,516]{0,1:T(8,128)} reshape(f32[2,704,516]{1,0,2:T(2,128)} %copy.22) | data formatting | bytes 5812224 | tf_op jit(solution)/shard_map/convert_element_type | solution.py:80
  41.0 2.4 multiply_reduce_fusion
  43.4 0.5 copy-done.1
  43.9 1.2 fusion.7
  45.1 3.0 %fusion.16 = f32[512,704]{0,1:T(8,128)S(1)} fusion(bf16[5,1408,704]{1,2,0:T(8,128)(2,1)} %param.11, bf16[516,1408]{1,0:T(8,128)(2,1)S(1)} %fusion.7), kind=kOutput, calls=%fused_computation.21 | convolution fusion | flops 1015021568 | bytes 4866048 | tf_op jit(solution)/shard_map/dot_general | solution.py:84
  48.2 1.4 copy-done.5
  49.6 1.3 fusion.12
  50.9 1.3 fusion.10
  52.2 1.3 fusion.8
  53.6 1.5 add_add_fusion
  55.1 1.6 copy.23
  56.7 1.8 reshape.55
  58.5 0.9 reduce_sum.46
  59.4 27.2 %all-gather.6.cloned.1.call-done = bf16[704,1536]{0,1:T(8,128)(2,1)} async-done(((bf16[704,192]{0,1:T(8,128)(2,1)}), bf16[704,1536]{0,1:T(8,128)(2,1)}) %all-gather.6.cloned.1.call-update) | async-done | bytes 2162704 | tf_op jit(solution)/shard_map/all_gather | solution.py:90
  86.6 3.3 %convolution_convert_fusion.1 = bf16[128,1536]{1,0:T(8,128)(2,1)} fusion(bf16[704,1536]{0,1:T(8,128)(2,1)} %all-gather.6.cloned.1.call-done, f32[128,704]{1,0:T(8,128)S(1)} %reduce_sum.46), kind=kOutput, calls=%fused_computation.11 | convolution fusion | flops 277200896 | bytes 2916352 | tf_op jit(solution)/shard_map/dot_general | solution.py:93
  89.9 1.3 stack.2
  91.2 3.7 %all-to-all-start = ((bf16[8,192,512]{2,1,0:T(8,128)(2,1)}), bf16[8,192,512]{2,1,0:T(8,128)(2,1)S(1)}, u32[]{:S(2)}, u32[]{:S(2)}) async-start(bf16[8,192,512]{2,1,0:T(8,128)(2,1)} %stack.2), calls=%async_computation.1 | async-start | bytes 3145728 | tf_op jit(solution)/shard_map/all_to_all | solution.py:111
  95.0 0.8 constant_dynamic-slice_fusion
  95.9 73.4 %all_gather.30 = bf16[1536,320]{1,0:T(8,128)(2,1)S(1)} all-gather(bf16[192,320]{1,0:T(8,128)(2,1)} %param.16), channel_id=1, replica_groups=mesh['grp'=2,'seq'=8,'col'=2] {'seq'}, dimensions={0}, use_global_device_ids=true | all-gather | bytes 1105920 | tf_op jit(solution)/shard_map/all_gather | solution.py:117
  169.3 1.1 fusion.39
  170.4 1.1 fusion.41
  171.4 2.3 all_gather.29
  173.7 0.5 convolution_convert_fusion.2
  174.3 0.2 copy-done.2
  174.5 1.4 fusion.35
  175.8 0.1 reshape.57
  175.9 26.4 %all_gather.31 = bf16[1024,128]{0,1:T(8,128)(2,1)S(1)} all-gather(bf16[128,128]{0,1:T(8,128)(2,1)S(1)} %slice.71), channel_id=1, replica_groups=mesh['grp'=2,'seq'=8,'col'=2] {'seq'}, dimensions={0}, use_global_device_ids=true | all-gather | bytes 294912 | tf_op jit(solution)/shard_map/all_gather | solution.py:126
  202.4 27.3 %all_gather.32 = bf16[1024,192]{0,1:T(8,128)(2,1)S(1)} all-gather(bf16[128,192]{0,1:T(8,128)(2,1)S(1)} %slice.72), channel_id=1, replica_groups=mesh['grp'=2,'seq'=8,'col'=2] {'seq'}, dimensions={0}, use_global_device_ids=true | all-gather | bytes 442368 | tf_op jit(solution)/shard_map/all_gather | solution.py:127
  229.7 0.5 fusion.57
  230.2 0.5 fusion.23
  230.7 0.6 fusion.34
  231.3 0.1 copy.24
  231.5 0.3 reshape.58
  231.8 3.3 %convolution_convert_fusion = bf16[128,1536]{1,0:T(8,128)(2,1)} fusion(bf16[128,768]{1,0:T(8,128)(2,1)S(1)} %reshape.58, bf16[768,1536]{0,1:T(8,128)(2,1)} %all-gather.8.cloned.1.call-done), kind=kOutput, calls=%fused_computation.10 | convolution fusion | flops 302186496 | bytes 2949120 | tf_op jit(solution)/shard_map/dot_general | solution.py:135
  235.1 5.2 %reduce-scatter.5.cloned.1.call-done = bf16[64,1536]{1,0:T(8,128)(2,1)} async-done(((bf16[128,1536]{1,0:T(8,128)(2,1)}), bf16[64,1536]{1,0:T(8,128)(2,1)}) %reduce-scatter.5.cloned.1.call-update) | async-done | bytes 196624 | tf_op jit(solution)/shard_map/reduce_scatter | solution.py:140
  240.4 1.7 convert_reduce_fusion
  242.0 0.2 fusion.36
  242.3 1.8 all-gather.1
  244.1 26.4 %all_gather.35 = bf16[64,128]{1,0:T(8,128)(2,1)S(1)} all-gather(bf16[8,128]{1,0:T(8,128)(2,1)S(1)} %get-tuple-element.7), channel_id=1, replica_groups=mesh['grp'=2,'seq'=8,'col'=2] {'seq'}, dimensions={0}, use_global_device_ids=true | all-gather | bytes 18432 | tf_op jit(solution)/shard_map/all_gather | solution.py:152
  270.6 0.8 convolution_convert_fusion.3
  (44 shorter events, 0.5 us)
Async XLA Ops:
  7.2 234.9 %copy-start = (bf16[1536,256]{1,0:T(8,128)(2,1)S(1)}, bf16[1536,256]{1,0:T(8,128)(2,1)}, u32[]{:S(2)}) copy-start(bf16[1536,256]{1,0:T(8,128)(2,1)} %param.18) | copy-start | bytes 2359300
  7.2 24.2 %all-gather.10.cloned.1.call-start = ((), (), s32[]{:S(2)}) async-start(), calls=%async_computation.7 | async-start | bytes 2396160 | tf_op jit(solution)/shard_map/all_gather | solution.py:78
  8.7 6.2 %collective-permute-start = (bf16[2,704]{1,0:T(2,128)(2,1)S(1)}, bf16[2,704]{1,0:T(2,128)(2,1)S(1)}, u32[]{:S(2)}, u32[]{:S(2)}) collective-permute-start(bf16[2,704]{1,0:T(2,128)(2,1)S(1)} %get-tuple-element.4), channel_id=1, source_target_pairs={{0,2},{2,4},{4,6},{6,8},{8,10},{10,12},{12,14},{1,3},{3,5},{5,7},{... | collective-permute-start | bytes 8456 | tf_op jit(solution)/shard_map/ppermute | solution.py:19
  13.6 5.5 %collective-permute-start.1 = (bf16[2,704]{1,0:T(2,128)(2,1)S(1)}, bf16[2,704]{1,0:T(2,128)(2,1)S(1)}, u32[]{:S(2)}, u32[]{:S(2)}) collective-permute-start(bf16[2,704]{1,0:T(2,128)(2,1)S(1)} %get-tuple-element.5), channel_id=1, source_target_pairs={{2,0},{4,2},{6,4},{8,6},{10,8},{12,10},{14,12},{3,1},{5,3},{7,5},{... | collective-permute-start | bytes 8456 | tf_op jit(solution)/shard_map/ppermute | solution.py:20
  20.2 66.3 %all-gather.6.cloned.1.call-start = ((), (), s32[]{:S(2)}) async-start(), calls=%async_computation.3 | async-start | bytes 2654208 | tf_op jit(solution)/shard_map/all_gather | solution.py:90
  21.0 148.3 %reduce-scatter.3.cloned.1.call-start = ((), (), s32[]{:S(2)}) async-start(), calls=%async_computation.4 | async-start | bytes 589824 | tf_op jit(solution)/shard_map/reduce_scatter | solution.py:92
  41.0 2.9 %copy-start.1 = (f32[1408,516]{0,1:T(8,128)S(1)}, f32[1408,516]{0,1:T(8,128)}, u32[]{:S(2)}) copy-start(f32[1408,516]{0,1:T(8,128)} %reshape.68) | copy-start | bytes 8718340
  41.0 2.9 %copy-start.9 = (f32[1408]{0:T(1024)S(1)}, f32[1408]{0:T(1024)}, u32[]{:S(2)}) copy-start(f32[1408]{0:T(1024)} %param.12) | copy-start | bytes 16900
  45.1 4.4 %copy-start.5 = (bf16[5,1408,704]{1,2,0:T(8,128)(2,1)S(1)}, bf16[5,1408,704]{1,2,0:T(8,128)(2,1)}, u32[]{:S(2)}) copy-start(bf16[5,1408,704]{1,2,0:T(8,128)(2,1)} %param.11) | copy-start | bytes 29736964
  52.2 1.4 copy-start.3
  59.4 30.5 %copy-start.7 = (bf16[192,1024]{1,0:T(8,128)(2,1)S(1)}, bf16[192,1024]{1,0:T(8,128)(2,1)}, u32[]{:S(2)}) copy-start(bf16[192,1024]{1,0:T(8,128)(2,1)} %param.15) | copy-start | bytes 1179652
  91.2 3.8 %copy-start.6 = (bf16[1536,192]{0,1:T(8,128)(2,1)S(1)}, bf16[1536,192]{0,1:T(8,128)(2,1)}, u32[]{:S(2)}) copy-start(bf16[1536,192]{0,1:T(8,128)(2,1)} %param.17) | copy-start | bytes 1769476
  91.2 83.2 %all-to-all-start = ((bf16[8,192,512]{2,1,0:T(8,128)(2,1)}), bf16[8,192,512]{2,1,0:T(8,128)(2,1)S(1)}, u32[]{:S(2)}, u32[]{:S(2)}) async-start(bf16[8,192,512]{2,1,0:T(8,128)(2,1)} %stack.2), calls=%async_computation.1 | async-start | bytes 3145728 | tf_op jit(solution)/shard_map/all_to_all | solution.py:111
  94.9 75.4 %copy-start.10 = (f32[1536]{0:T(1024)S(1)}, f32[1536]{0:T(1024)}, u32[]{:S(2)}) copy-start(f32[1536]{0:T(1024)} %param.14) | copy-start | bytes 18436
  95.0 136.8 %all-gather.8.cloned.1.call-start = ((), (), s32[]{:S(2)}) async-start(), calls=%async_computation.5 | async-start | bytes 2654208 | tf_op jit(solution)/shard_map/all_gather | solution.py:137
  95.8 144.6 %reduce-scatter.5.cloned.1.call-start = ((), (), s32[]{:S(2)}) async-start(), calls=%async_computation.6 | async-start | bytes 589824 | tf_op jit(solution)/shard_map/reduce_scatter | solution.py:140
  173.7 0.7 copy-start.2
  231.5 8.9 %copy-start.4 = (bf16[64,1536]{1,0:T(8,128)(2,1)S(1)}, bf16[64,1536]{1,0:T(8,128)(2,1)}, u32[]{:S(2)}) copy-start(bf16[64,1536]{1,0:T(8,128)(2,1)} %reduce-scatter.3.cloned.1.call-done) | copy-start | bytes 589828
  231.8 38.8 %copy-start.8 = (bf16[128,128]{1,0:T(8,128)(2,1)S(1)}, bf16[128,128]{1,0:T(8,128)(2,1)}, u32[]{:S(2)}) copy-start(bf16[128,128]{1,0:T(8,128)(2,1)} %param.19) | copy-start | bytes 98308
Sparse Core Ops, SparseCore 0:
  20.4 10.9 all-gather.9
  33.5 52.9 all-gather.5
  90.0 6.3 reduce-scatter.2
  98.4 83.7 all-gather.7
  235.2 5.0 reduce-scatter.4
